TPU v7x, 512 devices: a whole 4x4x16 slice. The times are simulated.
512 devices in a mesh: dp: 64 (over x, z_lo, core), mp: 8 (over y, z_hi).
Axes of the slice: x: 4, y: 4, z: 16 (z_hi: 2, z_lo: 8; z = z_hi * 8 + z_lo), core: 2. Of those that a mesh axis runs over, the one named last changes fastest.
Arguments:
- states: bfloat16 [128, 64, 2048], P('dp', None, 'mp'), may hold values from -6 to 6
- w_qkv: bfloat16 [3, 2048, 2048], P(None, 'dp', 'mp'), may hold values from -0.125 to 0.125
- w_out: bfloat16 [2048, 2048], P('dp', 'mp'), may hold values from -0.125 to 0.125
- cache_keys: bfloat16 [128, 384, 2048], P('dp', None, 'mp'), as said below
- cache_values: bfloat16 [128, 384, 2048], P('dp', None, 'mp'), may hold values from -6 to 6
- parents: int32 [128, 64], P('dp'), may hold values from 0 to 62, as said below
- accept: int32 [128, 8], P('dp'), may hold values from 0 to 63, as said below
- lengths: int32 [128], replicated, may hold values from 48 to 384
- perm: int32 [128], replicated, may hold values from 0 to 127, each once
Outputs:
- tree_out: bfloat16 [128, 64, 2048], P('dp', None, 'mp')
- new_keys: bfloat16 [128, 8, 2048], P('dp', None, 'mp')
- new_values: bfloat16 [128, 8, 2048], P('dp', None, 'mp')
Inputs may be any that keep to these rules, and one draw needn't show every extreme that they name: parents[r, 0] = 0 for the root and parents[r, i] < i for every other node. `accept`: each row is a chain of 8 nodes from the root (node 0) downward, each entry the parent of the next. `perm`: each request stands in exactly one slot. `cache_keys`: keys of earlier positions, already rotated; slots at or past the request's length hold arbitrary values.
All inputs are finite; a program needn't handle non-finite values.
Results may differ from a plain program's by a relative error of at most 0.012.
The roundings to bfloat16 on the way count: a program that leaves them out, or rounds other values in their place, can miss the bound.
Values may be sent and summed in bfloat16 or wider, within the bound.
A program may use at most 64 MiB of HBM per device.

v0:
```python
import jax
import jax.numpy as jnp
from jax import lax
from jax.sharding import PartitionSpec as P

HEAD_DIM = 128
EPSILON = 1e-05
ROPE_BASE = 10000.0
NEG_FILL = -1e30


def layer_norm(rows):
    mean_val = jnp.mean(rows, axis=-1, keepdims=True)
    centred = rows - mean_val
    variance = jnp.mean(centred * centred, axis=-1, keepdims=True)
    return centred * lax.rsqrt(variance + EPSILON)


def rotate(values, position):
    half = values.shape[-1] // 2
    freqs = ROPE_BASE ** (-(jnp.arange(half, dtype=jnp.float32) * 2.0 / values.shape[-1]))
    angle = position[:, :, None, None] * freqs
    cosine = jnp.cos(angle)
    sine = jnp.sin(angle)
    first = values[..., :half]
    second = values[..., half:]
    return jnp.concatenate(
        [first * cosine - second * sine, second * cosine + first * sine], axis=-1
    )


def closure(parents):
    tree_len = parents.shape[-1]
    node_ids = jnp.arange(tree_len, dtype=jnp.int32)
    linked = (parents[:, :, None] == node_ids[None, None, :]) & (node_ids[None, :, None] > 0)
    reach = jnp.eye(tree_len, dtype=jnp.float32)[None] + linked.astype(jnp.float32)
    covered = 1
    while covered < tree_len:
        reach = jnp.minimum(jnp.einsum("rij,rjk->rik", reach, reach), 1.0)
        covered = covered * 2
    return reach


def local(states, w_qkv, w_out, cache_keys, cache_values, parents, accept, lengths, perm):
    req_count, tree_len, local_dim = states.shape
    cache_len = cache_keys.shape[1]
    heads_here = local_dim // HEAD_DIM
    scale = HEAD_DIM ** (-0.5)
    flat_rows = req_count * tree_len
    gathered = lax.all_gather(states, "mp", axis=2, tiled=True)
    normed = layer_norm(gathered.astype(jnp.float32)).astype(jnp.bfloat16).reshape(flat_rows, -1)

    def add_one(piece):
        return jnp.dot(normed, piece, preferred_element_type=jnp.float32)

    query_flat = add_one(lax.all_gather(w_qkv[0], "dp", axis=0, tiled=True))
    key_flat = add_one(lax.all_gather(w_qkv[1], "dp", axis=0, tiled=True))
    value_flat = add_one(lax.all_gather(w_qkv[2], "dp", axis=0, tiled=True))
    dealt_ids = lax.dynamic_slice_in_dim(perm, lax.axis_index("dp") * req_count, req_count)
    matches = dealt_ids[:, None] == jnp.arange(perm.shape[0], dtype=jnp.int32)[None, :]
    own_lengths = jnp.sum(jnp.where(matches, lengths[None, :], 0), axis=1)
    reach = closure(parents)
    depth = jnp.sum(reach, axis=-1) - 1.0
    position = own_lengths.astype(jnp.float32)[:, None] + depth
    shape_heads = (req_count, tree_len, heads_here, HEAD_DIM)
    queries = rotate(query_flat.reshape(shape_heads), position).astype(jnp.bfloat16)
    keys_new = rotate(key_flat.reshape(shape_heads), position).astype(jnp.bfloat16)
    values_new = value_flat.reshape(shape_heads).astype(jnp.bfloat16)
    keys_old = cache_keys.reshape(req_count, cache_len, heads_here, HEAD_DIM)
    values_old = cache_values.reshape(req_count, cache_len, heads_here, HEAD_DIM)
    tree_scores = (
        jnp.einsum("rthd,rshd->rhts", queries, keys_new, preferred_element_type=jnp.float32) * scale
    )
    tree_scores = jnp.where(reach[:, None] > 0, tree_scores, NEG_FILL)
    cache_scores = (
        jnp.einsum("rthd,rchd->rhtc", queries, keys_old, preferred_element_type=jnp.float32) * scale
    )
    valid = jnp.arange(cache_len, dtype=jnp.int32)[None, :] < own_lengths[:, None]
    cache_scores = jnp.where(valid[:, None, None, :], cache_scores, NEG_FILL)
    peak = jnp.maximum(jnp.max(cache_scores, axis=-1), jnp.max(tree_scores, axis=-1))
    cache_exp = jnp.exp(cache_scores - peak[..., None])
    tree_exp = jnp.exp(tree_scores - peak[..., None])
    denom = jnp.sum(cache_exp, axis=-1) + jnp.sum(tree_exp, axis=-1)
    cache_prob = (cache_exp / denom[..., None]).astype(jnp.bfloat16)
    tree_prob = (tree_exp / denom[..., None]).astype(jnp.bfloat16)
    mixed = jnp.einsum(
        "rhtc,rchd->rthd", cache_prob, values_old, preferred_element_type=jnp.float32
    )
    mixed = mixed + jnp.einsum(
        "rhts,rshd->rthd", tree_prob, values_new, preferred_element_type=jnp.float32
    )
    attended = mixed.astype(jnp.bfloat16).reshape(flat_rows, local_dim)
    heads_all = lax.all_gather(attended, "mp", axis=1, tiled=True)
    projected_out = jnp.dot(
        heads_all,
        lax.all_gather(w_out, "dp", axis=0, tiled=True),
        preferred_element_type=jnp.float32,
    )
    tree_out = (
        states.astype(jnp.float32) + projected_out.reshape(req_count, tree_len, local_dim)
    ).astype(jnp.bfloat16)
    picker = (accept[:, :, None] == jnp.arange(tree_len, dtype=jnp.int32)[None, None, :]).astype(
        jnp.bfloat16
    )
    stacked = jnp.concatenate(
        [
            keys_new.reshape(req_count, tree_len, local_dim),
            values_new.reshape(req_count, tree_len, local_dim),
        ],
        axis=-1,
    )
    chosen = jnp.einsum("rdt,rtn->rdn", picker, stacked, preferred_element_type=jnp.float32).astype(
        jnp.bfloat16
    )
    return (tree_out, chosen[..., :local_dim], chosen[..., local_dim:])


def solution(mesh):
    in_specs = (
        P("dp", None, "mp"),
        P(None, "dp", "mp"),
        P("dp", "mp"),
        P("dp", None, "mp"),
        P("dp", None, "mp"),
        P("dp", None),
        P("dp", None),
        P(),
        P(),
    )
    out_specs = (P("dp", None, "mp"), P("dp", None, "mp"), P("dp", None, "mp"))
    return jax.shard_map(local, mesh=mesh, in_specs=in_specs, out_specs=out_specs, check_vma=False)
```

profile of v0, /device:TPU:33, one launch (start us, length us, event | category | flops | bytes accessed | tf_op | source)
XLA Modules:
  0.0 533.2 jit_solution(12800749686257656289)
XLA Ops:
  7.2 0.0 all-gather.14.cloned.1.call-start
  7.2 1.4 fusion.52
  8.7 0.0 all-gather.10.cloned.1.call-start
  8.7 0.7 all-gather.10.cloned.1.call-update
  9.5 0.7 all-gather.12.cloned.1.call-update
  10.2 0.5 all-gather.8.cloned.1.call-update
  10.8 0.6 copy-done.6
  11.4 0.1 dynamic_slice.3
  11.5 0.6 copy-done.7
  12.1 0.2 fusion.45
  12.3 0.1 iota_compare_fusion.4
  12.3 83.0 %all_gather.18 = bf16[2,64,2048]{2,1,0:T(8,128)(2,1)S(1)} all-gather(bf16[2,64,256]{2,1,0:T(8,128)(2,1)S(1)} %copy-done.2), channel_id=1, replica_groups=mesh['dp'=64,'mp'=8] {'mp'}, dimensions={2}, use_global_device_ids=true | all-gather | bytes 589824 | tf_op jit(solution)/shard_map/all_gather | solution.py:50
  95.3 0.2 convert_reduce_fusion
  95.5 0.3 fusion.6
  95.8 0.7 copy-done.4
  96.5 0.4 convolution_minimum_fusion.4
  96.9 0.3 convolution_minimum_fusion.2
  97.2 0.4 fusion.54
  97.5 0.1 copy.33
  97.7 0.1 add_add_fusion
  97.7 0.3 multiply_cosine_fusion
  98.0 50.2 %all-gather.14.cloned.1.call-done = bf16[1,2048,256]{2,1,0:T(8,128)(2,1)} async-done(((bf16[1,32,256]{2,1,0:T(8,128)(2,1)}), bf16[1,2048,256]{2,1,0:T(8,128)(2,1)}) %all-gather.14.cloned.1.call-update) | async-done | bytes 1048592 | tf_op jit(solution)/shard_map/all_gather | solution.py:58
  148.3 1.5 copy.36
  149.7 122.3 %all-gather.10.cloned.1.call-done = bf16[1,2048,256]{2,1,0:T(8,128)(2,1)} async-done(((bf16[1,32,256]{2,1,0:T(8,128)(2,1)}), bf16[1,2048,256]{2,1,0:T(8,128)(2,1)}) %all-gather.10.cloned.1.call-update) | async-done | bytes 1048592 | tf_op jit(solution)/shard_map/all_gather | solution.py:56
  272.0 1.5 copy.29
  273.5 116.4 %all-gather.12.cloned.1.call-done = bf16[1,2048,256]{2,1,0:T(8,128)(2,1)} async-done(((bf16[1,32,256]{2,1,0:T(8,128)(2,1)}), bf16[1,2048,256]{2,1,0:T(8,128)(2,1)}) %all-gather.12.cloned.1.call-update) | async-done | bytes 1048592 | tf_op jit(solution)/shard_map/all_gather | solution.py:57
  389.9 2.3 copy.34
  392.2 0.5 fusion.42
  392.7 0.7 copy-done.1
  393.4 0.5 fusion.40
  393.9 0.1 subtract_convert_fusion
  394.0 0.1 multiply_subtract_fusion
  394.2 0.3 fusion.56
  394.4 0.4 fusion.55
  394.9 0.2 fusion.13
  395.1 0.5 convolution_convert_fusion
  395.6 0.2 convolution_bitcast_fusion.1
  395.9 0.8 copy-done.3
  396.6 0.3 fusion.5
  396.9 0.1 copy.38
  397.0 0.1 copy_bitcast_fusion.1
  397.1 66.5 %all_gather.22 = bf16[128,2048]{1,0:T(8,128)(2,1)S(1)} all-gather(bf16[128,256]{1,0:T(8,128)(2,1)S(1)} %bitcast.82), channel_id=1, replica_groups=mesh['dp'=64,'mp'=8] {'mp'}, dimensions={1}, use_global_device_ids=true | all-gather | bytes 589824 | tf_op jit(solution)/shard_map/all_gather | solution.py:93
  463.6 59.5 %all-gather.8.cloned.1.call-done = bf16[2048,256]{1,0:T(8,128)(2,1)} async-done(((bf16[32,256]{1,0:T(8,128)(2,1)}), bf16[2048,256]{1,0:T(8,128)(2,1)}) %all-gather.8.cloned.1.call-update) | async-done | bytes 1048592 | tf_op jit(solution)/shard_map/all_gather | solution.py:96
  523.0 1.5 fusion.58
  524.6 0.6 add_convert_fusion
  525.2 0.7 copy-done.5
  525.9 0.2 convolution_convert_fusion.1
  526.1 0.6 fusion.53
  (24 shorter events, 0.2 us)
Async XLA Ops:
  7.2 387.3 %copy-start = (bf16[2,384,256]{2,1,0:T(8,128)(2,1)S(1)}, bf16[2,384,256]{2,1,0:T(8,128)(2,1)}, u32[]{:S(2)}) copy-start(bf16[2,384,256]{2,1,0:T(8,128)(2,1)} %param.12) | copy-start | bytes 1179652
  7.2 141.1 %all-gather.14.cloned.1.call-start = ((), (), s32[]{:S(2)}) async-start(), calls=%async_computation.3 | async-start | bytes 1064960 | tf_op jit(solution)/shard_map/all_gather | solution.py:58
  8.6 3.7 copy-start.2
  8.7 263.3 %all-gather.10.cloned.1.call-start = ((), (), s32[]{:S(2)}) async-start(), calls=%async_computation.1 | async-start | bytes 1064960 | tf_op jit(solution)/shard_map/all_gather | solution.py:56
  9.4 380.5 %all-gather.12.cloned.1.call-start = ((), (), s32[]{:S(2)}) async-start(), calls=%async_computation.2 | async-start | bytes 1064960 | tf_op jit(solution)/shard_map/all_gather | solution.py:57
  10.1 512.9 %all-gather.8.cloned.1.call-start = ((), (), s32[]{:S(2)}) async-start(), calls=%async_computation | async-start | bytes 1064960 | tf_op jit(solution)/shard_map/all_gather | solution.py:96
  10.8 0.7 copy-start.6
  11.4 0.7 copy-start.7
  95.8 0.7 copy-start.4
  392.2 1.2 copy-start.1
  395.6 1.0 copy-start.3
  525.2 0.7 copy-start.5
Sparse Core Ops, SparseCore 0:
  10.1 138.0 all-gather.13
  151.0 120.9 all-gather.9
  274.2 115.7 all-gather.11
  391.9 131.0 all-gather.7
where the time goes:
time: 534 us; the launch traced here: 533 us
  waiting for transfers between devices  350 us (66%)
  blocking collectives  149 us (28%)
  between operations  14 us (3%)
  local copies, waits for them, and re-layouts  11.6 us (2%)
  matrix products  5.43 us (1%)
    all_gather x1, waiting for transfers between devices, local(): query_flat = add_one(lax.all_gather(w_qkv[0], 'dp', axis=0, tiled=True))  122 us
    all_gather x1, waiting for transfers between devices, local(): key_flat = add_one(lax.all_gather(w_qkv[1], 'dp', axis=0, tiled=True))  116 us
    all_gather x1, blocking collectives, local(): gathered = lax.all_gather(states, 'mp', axis=2, tiled=True)  83 us
    all_gather x1, blocking collectives, local(): heads_all = lax.all_gather(attended, 'mp', axis=1, tiled=True)  66.5 us
    all_gather x1, waiting for transfers between devices, local(): lax.all_gather(w_out, 'dp', axis=0, tiled=True)  59.5 us
    all_gather x1, waiting for transfers between devices, local(): value_flat = add_one(lax.all_gather(w_qkv[2], 'dp', axis=0, tiled=True))  50.2 us
  transfers between devices with their start and end apart: 4, of which 4 were waited for; matrix products, arithmetic and copies ran while one was open for 2% of the time, Pallas kernels for 0%

commit v1 on v0

--- a/solution.py
+++ b/solution.py
@@ -54,7 +54,11 @@
         return jnp.dot(normed, piece, preferred_element_type=jnp.float32)
 
     query_flat = add_one(lax.all_gather(w_qkv[0], "dp", axis=0, tiled=True))
-    key_flat = add_one(lax.all_gather(w_qkv[1], "dp", axis=0, tiled=True))
+    key_flat = add_one(
+        jnp.concatenate(
+            lax.all_to_all(jnp.stack([w_qkv[1]] * lax.axis_size("dp")), "dp", 0, 0), axis=0
+        )
+    )
     value_flat = add_one(lax.all_gather(w_qkv[2], "dp", axis=0, tiled=True))
     dealt_ids = lax.dynamic_slice_in_dim(perm, lax.axis_index("dp") * req_count, req_count)
     matches = dealt_ids[:, None] == jnp.arange(perm.shape[0], dtype=jnp.int32)[None, :]

time: 534 us -> 419 us (0.78)
  the two profiles are of different devices: /device:TPU:33 before, /device:TPU:1 now
where the time goes in v1:
time: 419 us; the launch traced here: 418 us
  waiting for transfers between devices  215 us (51%)
  blocking collectives  148 us (35%)
  starting transfers between devices  17.2 us (4%)
  between operations  14.1 us (3%)
  local copies, waits for them, and re-layouts  13 us (3%)
  matrix products  8.59 us (2%)
    all_gather x1, waiting for transfers between devices, local(): query_flat = add_one(lax.all_gather(w_qkv[0], 'dp', axis=0, tiled=True))  121 us
    all_gather x1, blocking collectives, local(): heads_all = lax.all_gather(attended, 'mp', axis=1, tiled=True)  75.9 us
    all_gather x1, blocking collectives, local(): gathered = lax.all_gather(states, 'mp', axis=2, tiled=True)  72.2 us
    all_gather x1, waiting for transfers between devices, local(): value_flat = add_one(lax.all_gather(w_qkv[2], 'dp', axis=0, tiled=True))  48.2 us
    all_gather x1, waiting for transfers between devices, local(): lax.all_gather(w_out, 'dp', axis=0, tiled=True)  44.4 us
    all_to_all x1, starting transfers between devices, local(): lax.all_to_all(jnp.stack([w_qkv[1]] * lax.axis_size('dp')), 'dp', 0, 0)  17 us
  transfers between devices with their start and end apart: 4, of which 3 were waited for; matrix products, arithmetic and copies ran while one was open for 3% of the time, Pallas kernels for 0%

profile of v1, /device:TPU:1, one launch (start us, length us, event | category | flops | bytes accessed | tf_op | source)
XLA Modules:
  0.0 418.0 jit_solution(2629794247365147682)
XLA Ops:
  7.2 1.4 fusion.52
  8.7 0.7 all-gather.8.cloned.1.call-update
  9.4 1.1 stack.3
  10.5 17.0 %all-to-all-start = ((bf16[64,32,256]{2,1,0:T(8,128)(2,1)}), bf16[64,32,256]{2,1,0:T(8,128)(2,1)S(1)}, u32[]{:S(2)}, u32[]{:S(2)}) async-start(bf16[64,32,256]{2,1,0:T(8,128)(2,1)} %stack.3), calls=%async_computation | async-start | bytes 2097152 | tf_op jit(solution)/shard_map/all_to_all | solution.py:59
  27.6 0.7 all-gather.6.cloned.1.call-update
  28.3 0.6 copy-done.15
  29.0 0.1 dynamic_slice.3
  29.1 0.6 copy-done.16
  29.6 0.2 fusion.45
  29.9 0.7 copy-done.13
  30.5 0.4 convolution_minimum_fusion.4
  30.9 0.3 convolution_minimum_fusion.2
  31.2 0.4 fusion.54
  31.6 0.1 copy.33
  31.7 0.7 copy-done.5
  32.4 72.2 %all_gather.15 = bf16[2,64,2048]{2,1,0:T(8,128)(2,1)S(1)} all-gather(bf16[2,64,256]{2,1,0:T(8,128)(2,1)S(1)} %copy-done.5), channel_id=1, replica_groups=mesh['dp'=64,'mp'=8] {'mp'}, dimensions={2}, use_global_device_ids=true | all-gather | bytes 589824 | tf_op jit(solution)/shard_map/all_gather | solution.py:50
  104.6 0.2 convert_reduce_fusion
  104.8 0.3 fusion.6
  105.0 0.1 iota_compare_fusion.4
  105.1 0.1 add_add_fusion
  105.2 0.3 multiply_cosine_fusion
  105.5 48.2 %all-gather.10.cloned.1.call-done = bf16[1,2048,256]{2,1,0:T(8,128)(2,1)} async-done(((bf16[1,32,256]{2,1,0:T(8,128)(2,1)}), bf16[1,2048,256]{2,1,0:T(8,128)(2,1)}) %all-gather.10.cloned.1.call-update) | async-done | bytes 1048592 | tf_op jit(solution)/shard_map/all_gather | solution.py:62
  153.7 1.5 copy.36
  155.2 120.9 %all-gather.8.cloned.1.call-done = bf16[1,2048,256]{2,1,0:T(8,128)(2,1)} async-done(((bf16[1,32,256]{2,1,0:T(8,128)(2,1)}), bf16[1,2048,256]{2,1,0:T(8,128)(2,1)}) %all-gather.8.cloned.1.call-update) | async-done | bytes 1048592 | tf_op jit(solution)/shard_map/all_gather | solution.py:56
  276.1 2.3 copy.29
  278.3 1.7 fusion.42
  280.1 0.1 subtract_convert_fusion
  280.2 1.1 convolution_convert_fusion
  281.3 1.0 fusion.55
  282.3 0.6 copy.34
  283.0 0.7 copy-done.10
  283.7 1.2 fusion.40
  284.9 0.1 multiply_subtract_fusion
  285.0 0.3 fusion.56
  285.3 0.7 copy-done.8
  286.0 0.2 fusion.13
  286.3 0.6 copy-done.7
  286.8 0.2 convolution_bitcast_fusion.1
  287.1 0.3 fusion.5
  287.4 0.1 copy.38
  287.5 0.1 copy_bitcast_fusion.1
  287.6 75.9 %all_gather.18 = bf16[128,2048]{1,0:T(8,128)(2,1)S(1)} all-gather(bf16[128,256]{1,0:T(8,128)(2,1)S(1)} %bitcast.84), channel_id=1, replica_groups=mesh['dp'=64,'mp'=8] {'mp'}, dimensions={1}, use_global_device_ids=true | all-gather | bytes 589824 | tf_op jit(solution)/shard_map/all_gather | solution.py:97
  363.4 44.4 %all-gather.6.cloned.1.call-done = bf16[2048,256]{1,0:T(8,128)(2,1)} async-done(((bf16[32,256]{1,0:T(8,128)(2,1)}), bf16[2048,256]{1,0:T(8,128)(2,1)}) %all-gather.6.cloned.1.call-update) | async-done | bytes 1048592 | tf_op jit(solution)/shard_map/all_gather | solution.py:100
  407.8 1.5 fusion.58
  409.3 0.6 add_convert_fusion
  410.0 0.7 copy-done.14
  410.6 0.2 convolution_convert_fusion.1
  410.8 0.6 fusion.53
  (42 shorter events, 0.3 us)
Async XLA Ops:
  7.2 274.2 %copy-start = (bf16[2,384,256]{2,1,0:T(8,128)(2,1)S(1)}, bf16[2,384,256]{2,1,0:T(8,128)(2,1)}, u32[]{:S(2)}) copy-start(bf16[2,384,256]{2,1,0:T(8,128)(2,1)} %param.12) | copy-start | bytes 1179652
  7.2 146.5 %all-gather.10.cloned.1.call-start = ((), (), s32[]{:S(2)}) async-start(), calls=%async_computation.3 | async-start | bytes 1064960 | tf_op jit(solution)/shard_map/all_gather | solution.py:62
  8.7 267.4 %all-gather.8.cloned.1.call-start = ((), (), s32[]{:S(2)}) async-start(), calls=%async_computation.2 | async-start | bytes 1064960 | tf_op jit(solution)/shard_map/all_gather | solution.py:56
  10.5 271.8 %all-to-all-start = ((bf16[64,32,256]{2,1,0:T(8,128)(2,1)}), bf16[64,32,256]{2,1,0:T(8,128)(2,1)S(1)}, u32[]{:S(2)}, u32[]{:S(2)}) async-start(bf16[64,32,256]{2,1,0:T(8,128)(2,1)} %stack.3), calls=%async_computation | async-start | bytes 2097152 | tf_op jit(solution)/shard_map/all_to_all | solution.py:59
  27.6 380.2 %all-gather.6.cloned.1.call-start = ((), (), s32[]{:S(2)}) async-start(), calls=%async_computation.1 | async-start | bytes 1064960 | tf_op jit(solution)/shard_map/all_gather | solution.py:100
  28.3 0.7 copy-start.15
  29.0 0.7 copy-start.16
  29.8 0.7 copy-start.13
  31.6 0.8 copy-start.5
  104.8 175.4 %copy-start.9 = (f32[2,64]{1,0:T(2,128)}, f32[2,64]{1,0:T(2,128)S(1)}, u32[]{:S(2)}) copy-start(f32[2,64]{1,0:T(2,128)S(1)} %broadcast_multiply_fusion) | copy-start | bytes 1540
  105.1 175.0 %copy-start.11 = (f32[2,64]{1,0:T(2,128)}, f32[2,64]{1,0:T(2,128)S(1)}, u32[]{:S(2)}) copy-start(f32[2,64]{1,0:T(2,128)S(1)} %add_rsqrt_fusion) | copy-start | bytes 1540
  105.5 174.5 %copy-start.1 = (f32[2,64,64]{2,1,0:T(8,128)}, f32[2,64,64]{2,1,0:T(8,128)S(1)}, u32[]{:S(2)}) copy-start(f32[2,64,64]{2,1,0:T(8,128)S(1)} %get-tuple-element.12) | copy-start | bytes 98308
  105.5 174.5 %copy-start.3 = (f32[2,64,64]{2,1,0:T(8,128)}, f32[2,64,64]{2,1,0:T(8,128)S(1)}, u32[]{:S(2)}) copy-start(f32[2,64,64]{2,1,0:T(8,128)S(1)} %get-tuple-element.13) | copy-start | bytes 98308
  283.0 0.7 copy-start.10
  283.7 1.2 copy-start.2
  283.7 1.2 copy-start.4
  285.3 0.7 copy-start.8
  286.0 0.8 copy-start.7
  286.0 1.0 copy-start.12
  363.4 45.9 %copy-start.6 = (bf16[2,64,256]{2,1,0:T(8,128)(2,1)S(1)}, bf16[2,64,256]{2,1,0:T(8,128)(2,1)}, u32[]{:S(2)}) copy-start(bf16[2,64,256]{2,1,0:T(8,128)(2,1)} %param.9) | copy-start | bytes 196612
  410.0 0.7 copy-start.14
Sparse Core Ops, SparseCore 0:
  10.1 143.5 all-gather.9
  156.4 119.5 all-gather.7
  278.2 129.5 all-gather.5
